TPU v7x, 32 devices: a whole 2x2x4 slice. The times are simulated.
32 devices in a mesh: view: 8 (over z, x), head: 4 (over y, core).
Axes of the slice: x: 2, y: 2, z: 4, core: 2. Of those that a mesh axis runs over, the one named last changes fastest.
Arguments:
- features: bfloat16 [16384, 1024], P(('view', 'head')), may hold values from -6 to 6
- attend_weight: bfloat16 [2, 3, 1024, 1024], P(None, None, 'view', 'head'), may hold values from -0.1875 to 0.1875
- output_weight: bfloat16 [2, 1024, 1024], P(None, 'view'), may hold values from -0.1875 to 0.1875
- fast_init: bfloat16 [2, 16, 3, 64, 512], P(None, 'head', None, None, 'view'), may hold values from -0.75 to 0.75
- update_mask: int32 [8, 2048], P('view'), may hold values 0 or 1
Outputs:
- refined: bfloat16 [16384, 1024], P(('view', 'head'))
All inputs are finite; a program needn't handle non-finite values. No bound on the sum of `update_mask` on one device may be relied on, other than what follows from the above.
Results may differ from a plain program's by a relative error of at most 0.035.
Values may be sent and summed in bfloat16 or wider, within the bound.
No kernel may reach another device: no remote copies, remote signals or barrier semaphores. Data moves between devices by JAX's collectives and lax.ppermute only.
A program may use at most 64 MiB of HBM per device.

v0:
```python
import jax
import jax.numpy as jnp
from jax import lax
from jax.sharding import PartitionSpec as P

BLOCKS = 2
NS_STEPS = 5
newton_coeffs = (3.4445, -4.775, 2.0315)
learn_rate = 1.0
score_scale = 0.25


def normalize(values, epsilon):
    return values * lax.rsqrt(jnp.mean(values * values, axis=-1, keepdims=True) + epsilon)


def newton_step(current, gram_matrix):
    squared = jnp.einsum(
        "...de,...ef->...df", gram_matrix, gram_matrix, precision=lax.Precision.HIGHEST
    )
    polynomial = newton_coeffs[1] * gram_matrix + newton_coeffs[2] * squared
    return newton_coeffs[0] * current + jnp.einsum(
        "...de,...ef->...df", polynomial, current, precision=lax.Precision.HIGHEST
    )


def self_gram(current):
    return jnp.einsum("...df,...ef->...de", current, current, precision=lax.Precision.HIGHEST)


def fast_gradient(keys, values, mask, weights):
    first = jnp.einsum("thd,hdf->thf", keys, weights[:, 0], preferred_element_type=jnp.float32)
    third = jnp.einsum("thd,hdf->thf", keys, weights[:, 1], preferred_element_type=jnp.float32)
    sigma = jax.nn.sigmoid(first)
    hidden = (first * sigma * third).astype(jnp.bfloat16)
    target = (-(mask[:, None, None].astype(jnp.float32) * values.astype(jnp.float32))).astype(
        jnp.bfloat16
    )
    back = jnp.einsum("thd,hdf->thf", target, weights[:, 2], preferred_element_type=jnp.float32)
    d_third = (back * first * sigma).astype(jnp.bfloat16)
    d_first = (back * third * sigma * (1.0 + first * (1.0 - sigma))).astype(jnp.bfloat16)
    grad_first = jnp.einsum("thd,thf->hdf", keys, d_first, preferred_element_type=jnp.float32)
    grad_third = jnp.einsum("thd,thf->hdf", keys, d_third, preferred_element_type=jnp.float32)
    grad_last = jnp.einsum("thd,thf->hdf", target, hidden, preferred_element_type=jnp.float32)
    return jnp.stack([grad_first, grad_third, grad_last], axis=1)


def fast_apply(queries, weights):
    first = jnp.einsum("thd,hdf->thf", queries, weights[:, 0], preferred_element_type=jnp.float32)
    third = jnp.einsum("thd,hdf->thf", queries, weights[:, 1], preferred_element_type=jnp.float32)
    hidden = (first * jax.nn.sigmoid(first) * third).astype(jnp.bfloat16)
    output = jnp.einsum("thf,hdf->thd", hidden, weights[:, 2], preferred_element_type=jnp.float32)
    return normalize(output, 1e-05)


def shards(features, attend_weight, output_weight, fast_init, update_mask):
    stream = features
    view_dev, view_len = update_mask.shape
    heads_here = fast_init.shape[1]
    head_dim = fast_init.shape[3]
    rows_all = view_dev * view_len
    block = min(512, view_len)
    count = rows_all // block
    mask_blocks = update_mask.reshape(count, block)
    for layer in range(BLOCKS):
        normed = normalize(stream.astype(jnp.float32), 1e-05).astype(jnp.bfloat16)
        whole = lax.all_gather(normed, "head", axis=0, tiled=True)
        packed = jnp.einsum(
            "td,jdc->tjc",
            whole,
            lax.all_gather(attend_weight[layer], "view", axis=1, tiled=True),
            preferred_element_type=jnp.float32,
        ).astype(jnp.bfloat16)
        packed = packed.reshape(rows_all, 3, heads_here, head_dim)
        queries = normalize(packed[:, 0].astype(jnp.float32), 1e-05).astype(jnp.bfloat16)
        keys = normalize(packed[:, 1].astype(jnp.float32), 1e-05).astype(jnp.bfloat16)
        values = packed[:, 2]
        key_views = keys.reshape(view_dev, view_len, heads_here, head_dim)
        value_views = values.reshape(view_dev, view_len, heads_here, head_dim)
        query_blocks = jnp.moveaxis(
            queries.reshape(view_dev, view_len // block, block, heads_here, head_dim), 1, 0
        )

        def attend_block(query_block):
            scores = (
                jnp.einsum(
                    "vqhd,vkhd->vhqk", query_block, key_views, preferred_element_type=jnp.float32
                )
                * score_scale
            )
            expo = jnp.exp(scores)
            probs = (expo / jnp.sum(expo, axis=-1, keepdims=True)).astype(jnp.bfloat16)
            return jnp.einsum(
                "vhqk,vkhd->vqhd", probs, value_views, preferred_element_type=jnp.float32
            )

        attended = jnp.moveaxis(lax.map(attend_block, query_blocks), 0, 1).reshape(
            rows_all, heads_here, head_dim
        )
        local_fast = fast_init[layer]
        full_fast = lax.all_gather(local_fast, "view", axis=3, tiled=True)

        def accumulate(total, inputs):
            return (total + fast_gradient(inputs[0], inputs[1], inputs[2], full_fast), None)

        key_blocks = keys.reshape(count, block, heads_here, head_dim)
        value_blocks = values.reshape(count, block, heads_here, head_dim)
        gradients, _ = lax.scan(
            accumulate,
            jnp.zeros(full_fast.shape, jnp.float32),
            (key_blocks, value_blocks, mask_blocks),
        )
        summed = lax.psum(gradients.astype(jnp.bfloat16), "view").astype(jnp.float32)
        squares = jnp.sum(summed * summed, axis=(2, 3), keepdims=True)
        current = summed * lax.rsqrt(squares + 1e-06)
        for _ in range(NS_STEPS):
            current = newton_step(current, self_gram(current))
        updated = (full_fast.astype(jnp.float32) - learn_rate * current).astype(jnp.bfloat16)

        def apply_block(query_block):
            return fast_apply(query_block, updated)

        applied = lax.map(apply_block, queries.reshape(count, block, heads_here, head_dim)).reshape(
            rows_all, heads_here, head_dim
        )
        mixed = (attended + applied).astype(jnp.bfloat16).reshape(rows_all, heads_here * head_dim)
        regrouped = lax.all_to_all(mixed, "head", split_axis=0, concat_axis=1, tiled=True)
        projected = jnp.dot(
            regrouped,
            lax.all_gather(output_weight[layer], "view", axis=0, tiled=True),
            preferred_element_type=jnp.float32,
        )
        stream = (stream.astype(jnp.float32) + projected).astype(jnp.bfloat16)
    return stream


def solution(mesh):
    return jax.shard_map(
        shards,
        mesh=mesh,
        in_specs=(
            P(("view", "head"), None),
            P(None, None, "view", "head"),
            P(None, "view", None),
            P(None, "head", None, None, "view"),
            P("view", None),
        ),
        out_specs=P(("view", "head"), None),
        check_vma=False,
    )
```

profile of v0, /device:TPU:0, one launch (start us, length us, event | category | flops | bytes accessed | tf_op | source)
XLA Modules:
  0.0 636.8 jit_solution(1773703120889669409)
XLA Ops:
  11.7 44.0 %all-gather.1 = bf16[1,4,3,64,512]{3,1,2,0,4:T(4,128)(2,1)} all-gather(bf16[1,4,3,64,64]{3,1,2,0,4:T(4,128)(2,1)S(1)} %copy.61), channel_id=3, replica_groups=mesh['view'=8,'head'=4] {'view'}, dimensions={4}, use_global_device_ids=true | all-gather | bytes 884736 | tf_op jit(solution)/shard_map/all_gather | solution.py:101
  59.5 6.3 all-gather.17.cloned.1.call-done
  65.8 35.9 %all-gather.13.cloned.1.call-done = bf16[2048,1024]{1,0:T(8,128)(2,1)} async-done(((bf16[512,1024]{1,0:T(8,128)(2,1)}), bf16[2048,1024]{1,0:T(8,128)(2,1)}) %all-gather.13.cloned.1.call-update) | async-done | bytes 4194320 | tf_op jit(solution)/shard_map/all_gather | solution.py:67
  101.7 6.1 fusion.188
  122.1 60.1 %while.66 = (s32[]{:T(128)}, f32[4,3,64,512]{3,2,0,1:T(8,128)S(1)}, bf16[4,512,4,64]{1,3,2,0:T(8,128)(2,1)}, s32[4,512]{1,0:T(4,128)S(1)}, bf16[4,512,4,64]{1,3,...) while((s32[]{:T(128)}, f32[4,3,64,512]{3,2,0,1:T(8,128)S(1)}, ...), condition=%wide.region_7.8_spmd.clone, body=%wide.region_6.7_spmd.clone.sunk | while | flops 830996992 | bytes 50605152 | solution.py:108
  199.0 31.0 %while.62 = (s32[]{:T(128)}, f32[4,1,512,4,64]{2,4,3,1,0:T(8,128)S(1)}, bf16[4,1,512,4,64]{2,4,3,1,0:T(8,128)(2,1)}, bf16[1,2048,4,64]{1,3,2,0:T(8,128)(2,1)S(1)}, bf16[1,2048,4,64]{1,3,2,0:T(8,128)(2,1)}, /*index=5*/s32[]{:T(128)}) while((s32[]{:T(128)}, f32[4,1,512,4,64]{2,4,3,1,0:T(8,128)S(1)}, bf16[4,1,512,4,64]{2,4,3,1,0:T(8,128)(2,1)}, ...), condition=%wide.region_5.6_spmd, body=%wide.region_3.5_spmd.sunk | while | flops 1094711296 | bytes 40649316 | solution.py:97
  199.0 4.0 fusion.368
  206.8 4.0 fusion.368
  230.0 28.5 %all-reduce.3.cloned.1.call-done = bf16[4,3,64,512]{3,2,1,0:T(8,128)(2,1)} async-done(((bf16[4,3,64,512]{3,2,1,0:T(8,128)(2,1)}), bf16[4,3,64,512]{3,2,1,0:T(8,128)(2,1)}) %all-reduce.3.cloned.1.call-update) | async-done | bytes 786448 | tf_op jit(solution)/shard_map/psum | solution.py:113
  283.2 35.3 %while.63 = (s32[]{:T(128)}, f32[4,512,4,64]{1,3,2,0:T(8,128)}, bf16[4,512,4,64]{1,3,2,0:T(8,128)(2,1)}, bf16[4,3,64,512]{3,2,0,1:T(8,128)(2,1)}, s32[]{:T(128)}) while((s32[]{:T(128)}, f32[4,512,4,64]{1,3,2,0:T(8,128)}, bf16[4,512,4,64]{1,3,2,0:T(8,128)(2,1)}, bf16[4,3,64,512]{3,2,0,1:T(8,128)(2,1)}, s32[]{:T(128)}) %tuple.131), condition=%wide.region_12.13_spmd, body=%wide.region_10.12_spmd.sunk | while | flops 409339904 | bytes 11306557 | solution.py:123
  287.0 4.1 multiply_reduce_fusion.8
  295.8 4.2 multiply_reduce_fusion.8
  304.6 4.1 multiply_reduce_fusion.8
  313.4 4.2 multiply_reduce_fusion.8
  325.1 14.3 %all-to-all-done = bf16[4,512,256]{1,2,0:T(8,128)(2,1)S(1)} async-done(((bf16[4,512,256]{1,2,0:T(8,128)(2,1)}), bf16[4,512,256]{1,2,0:T(8,128)(2,1)S(1)}, u32[]{:S(2)}, u32[]{:S(2)}) %all-to-all-start) | async-done | bytes 1048608 | tf_op jit(solution)/shard_map/all_to_all | solution.py:127
  344.9 38.5 %all-gather.4 = bf16[1,4,3,64,512]{3,1,2,0,4:T(4,128)(2,1)} all-gather(bf16[1,4,3,64,64]{3,1,2,0,4:T(4,128)(2,1)S(1)} %copy.63), channel_id=6, replica_groups=mesh['view'=8,'head'=4] {'view'}, dimensions={4}, use_global_device_ids=true | all-gather | bytes 884736 | tf_op jit(solution)/shard_map/all_gather | solution.py:101
  386.2 5.2 all-gather.15.cloned.1.call-done
  391.5 6.1 fusion.191
  411.8 62.9 %while.67 = (s32[]{:T(128)}, f32[4,3,64,512]{3,2,0,1:T(8,128)S(1)}, bf16[4,512,4,64]{1,3,2,0:T(8,128)(2,1)}, s32[4,512]{1,0:T(4,128)}, bf16[4,512,4,64]{1,3,2,0:...) while((s32[]{:T(128)}, f32[4,3,64,512]{3,2,0,1:T(8,128)S(1)}, ...), condition=%wide.region_20.21_spmd.clone, body=%wide.region_19.20_spmd.clone.sunk | while | flops 830996992 | bytes 50605152 | solution.py:108
  491.3 34.0 %while.64 = (s32[]{:T(128)}, f32[4,1,512,4,64]{2,4,3,1,0:T(8,128)}, bf16[4,1,512,4,64]{2,4,3,1,0:T(8,128)(2,1)}, bf16[1,2048,4,64]{1,3,2,0:T(8,128)(2,1)S(1)}, bf16[1,2048,4,64]{1,3,2,0:T(8,128)(2,1)}, /*index=5*/s32[]{:T(128)}) while((s32[]{:T(128)}, f32[4,1,512,4,64]{2,4,3,1,0:T(8,128)}, bf16[4,1,512,4,64]{2,4,3,1,0:T(8,128)(2,1)}, ...), condition=%wide.region_18.19_spmd, body=%wide.region_16.18_spmd.sunk | while | flops 1094711296 | bytes 40649824 | solution.py:97
  491.3 4.1 fusion.376
  495.4 4.3 fusion.377
  503.8 4.3 fusion.377
  512.2 4.3 fusion.377
  520.5 4.3 fusion.377
  526.9 24.3 %all-reduce.5.cloned.1.call-done = bf16[4,3,64,512]{3,2,1,0:T(8,128)(2,1)} async-done(((bf16[4,3,64,512]{3,2,1,0:T(8,128)(2,1)}), bf16[4,3,64,512]{3,2,1,0:T(8,128)(2,1)}) %all-reduce.5.cloned.1.call-update) | async-done | bytes 786448 | tf_op jit(solution)/shard_map/psum | solution.py:113
  573.2 31.6 %while.65 = (s32[]{:T(128)}, f32[4,512,4,64]{1,3,2,0:T(8,128)S(1)}, bf16[4,512,4,64]{1,3,2,0:T(8,128)(2,1)}, bf16[4,3,64,512]{3,2,0,1:T(8,128)(2,1)S(1)}, s32[]{:T(128)}) while((s32[]{:T(128)}, f32[4,512,4,64]{1,3,2,0:T(8,128)S(1)}, bf16[4,512,4,64]{1,3,2,0:T(8,128)(2,1)}, bf16[4,3,64,512]{3,2,0,1:T(8,128)(2,1)S(1)}, s32[]{:T(128)}) %tuple.140), condition=%wide.region_25.26_spmd, body=%wide.region_23.25_spmd.sunk | while | flops 409339904 | bytes 11306049 | solution.py:123
  576.9 4.1 multiply_reduce_fusion.9
  584.8 4.1 multiply_reduce_fusion.9
  592.7 4.1 multiply_reduce_fusion.9
  600.6 4.1 multiply_reduce_fusion.9
  611.6 14.4 %all-to-all-done.1 = bf16[4,512,256]{1,2,0:T(8,128)(2,1)S(1)} async-done(((bf16[4,512,256]{1,2,0:T(8,128)(2,1)}), bf16[4,512,256]{1,2,0:T(8,128)(2,1)S(1)}, u32[]{:S(2)}, u32[]{:S(2)}) %all-to-all-start.1) | async-done | bytes 1048608 | tf_op jit(solution)/shard_map/all_to_all | solution.py:127
  (276 shorter events, 335.1 us)
Async XLA Ops:
  6.5 2.7 copy-start.7
  6.5 59.3 %all-gather.17.cloned.1.call-start = ((), (), s32[]{:S(2)}) async-start(), calls=%async_computation.6 | async-start | bytes 1769472 | tf_op jit(solution)/shard_map/all_gather | solution.py:71
  9.2 92.5 %all-gather.13.cloned.1.call-start = ((), (), s32[]{:S(2)}) async-start(), calls=%async_computation.2 | async-start | bytes 5242880 | tf_op jit(solution)/shard_map/all_gather | solution.py:67
  10.8 247.8 %all-reduce.3.cloned.1.call-start = ((), (), s32[]{:S(2)}) async-start(), calls=%async_computation.3 | async-start | bytes 1572864 | tf_op jit(solution)/shard_map/psum | solution.py:113
  11.7 47.1 %copy-start.22 = (s32[1,2048]{1,0:T(1,128)S(1)}, s32[1,2048]{1,0:T(1,128)}, u32[]{:S(2)}) copy-start(s32[1,2048]{1,0:T(1,128)} %param.21) | copy-start | bytes 24580
  107.9 3.3 copy-start.2
  182.3 2.2 copy-start.18
  183.3 5.4 copy-start
  183.3 141.8 %all-gather.19.cloned.1.call-start = ((), (), s32[]{:S(2)}) async-start(), calls=%async_computation.7 | async-start | bytes 2359296 | tf_op jit(solution)/shard_map/all_gather | solution.py:130
  184.3 202.0 %all-gather.21.cloned.1.call-start = ((), (), s32[]{:S(2)}) async-start(), calls=%async_computation.8 | async-start | bytes 1769472 | tf_op jit(solution)/shard_map/all_gather | solution.py:71
  199.0 4.1 copy-start.13
  206.8 4.1 copy-start.13
  214.5 4.1 copy-start.13
  222.3 4.1 copy-start.13
  258.6 5.3 copy-start.11
  276.9 2.1 copy-start.9
  321.4 18.1 %copy-start.8 = (bf16[512,1024]{1,0:T(8,128)(2,1)S(1)}, bf16[512,1024]{1,0:T(8,128)(2,1)}, u32[]{:S(2)}) copy-start(bf16[512,1024]{1,0:T(8,128)(2,1)} %param.17) | copy-start | bytes 3145732
  321.4 18.1 %all-to-all-start = ((bf16[4,512,256]{1,2,0:T(8,128)(2,1)}), bf16[4,512,256]{1,2,0:T(8,128)(2,1)S(1)}, u32[]{:S(2)}, u32[]{:S(2)}) async-start(bf16[4,512,256]{1,2,0:T(8,128)(2,1)} %fusion.206), calls=%async_computation | async-start | bytes 2097152 | tf_op jit(solution)/shard_map/all_to_all | solution.py:127
  325.1 66.4 %all-gather.15.cloned.1.call-start = ((), (), s32[]{:S(2)}) async-start(), calls=%async_computation.4 | async-start | bytes 5242880 | tf_op jit(solution)/shard_map/all_gather | solution.py:67
  342.4 2.3 copy-start.17
  344.7 206.5 %all-reduce.5.cloned.1.call-start = ((), (), s32[]{:S(2)}) async-start(), calls=%async_computation.5 | async-start | bytes 1572864 | tf_op jit(solution)/shard_map/psum | solution.py:113
  397.6 3.3 copy-start.3
  475.8 135.8 %all-gather.23.cloned.1.call-start = ((), (), s32[]{:S(2)}) async-start(), calls=%async_computation.9 | async-start | bytes 2359296 | tf_op jit(solution)/shard_map/all_gather | solution.py:130
  476.5 5.1 copy-start.1
  491.3 34.0 %copy-start.4 = (f32[4,512,4,64]{1,0,3,2:T(4,128)S(1)}, f32[4,512,4,64]{1,0,3,2:T(4,128)}, u32[]{:S(2)}) copy-start(f32[4,512,4,64]{1,0,3,2:T(4,128)} %reshape.326) | copy-start | bytes 6291460
  491.3 4.1 copy-start.14
  499.7 4.0 copy-start.14
  508.1 4.0 copy-start.14
  516.5 4.0 copy-start.14
  551.1 5.2 copy-start.12
  607.9 18.1 %copy-start.16 = (bf16[512,1024]{1,0:T(8,128)(2,1)S(1)}, bf16[512,1024]{1,0:T(8,128)(2,1)}, u32[]{:S(2)}) copy-start(bf16[512,1024]{1,0:T(8,128)(2,1)} %copy-done.15) | copy-start | bytes 3145732
  607.9 18.1 %all-to-all-start.1 = ((bf16[4,512,256]{1,2,0:T(8,128)(2,1)}), bf16[4,512,256]{1,2,0:T(8,128)(2,1)S(1)}, u32[]{:S(2)}, u32[]{:S(2)}) async-start(bf16[4,512,256]{1,2,0:T(8,128)(2,1)} %fusion.202), calls=%async_computation.1 | async-start | bytes 2097152 | tf_op jit(solution)/shard_map/all_to_all | solution.py:127
  (7 other events, 11.5 us)
Sparse Core Ops, SparseCore 0:
  9.4 56.3 all-gather.16
  67.4 34.3 all-gather.12
  183.4 75.1 all-reduce.2
  260.6 48.2 all-gather.18
  310.8 45.6 all-gather.20
  357.8 33.5 all-gather.14
  475.9 75.2 all-reduce.4
  553.2 48.2 all-gather.22
where the time goes:
time: 649 us; the launch traced here: 637 us
  matrix products  294 us (45%)
  waiting for transfers between devices  130 us (20%)
  blocking collectives  82.5 us (13%)
  local copies, waits for them, and re-layouts  56.3 us (9%)
  other arithmetic  50.9 us (8%)
  between operations  14.3 us (2%)
  starting transfers between devices  7.77 us (1%)
    all_gather x2, blocking collectives, shards(): full_fast = lax.all_gather(local_fast, 'view', axis=3, tiled=True)  82.5 us
    psum x2, waiting for transfers between devices, shards(): lax.psum(gradients.astype(jnp.bfloat16), 'view').astype(jnp.float32)  52.8 us
    all_gather x2, waiting for transfers between devices, shards(): whole = lax.all_gather(normed, 'head', axis=0, tiled=True)  41.2 us
    dot_general x8, matrix products, fast_apply(): jnp.einsum('thf,hdf->thd', hidden, weights[:, 2], preferred_element_type=...  33 us
    dot_general x8, matrix products, attend_block(): jnp.einsum('vqhd,vkhd->vhqk', query_block, key_views, preferred_element_t...  32.4 us
    dot_general x8, matrix products, attend_block(): jnp.einsum('vhqk,vkhd->vqhd', probs, value_views, preferred_element_type=...  31.9 us
    dot_general x8, matrix products, fast_apply(): jnp.einsum('thd,hdf->thf', queries, weights[:, 0], preferred_element_type...  29.9 us
    all_to_all x2, waiting for transfers between devices, shards(): lax.all_to_all(mixed, 'head', split_axis=0, concat_axis=1, tiled=True)  28.7 us
  transfers between devices with their start and end apart: 10, of which 7 were waited for; matrix products, arithmetic and copies ran while one was open for 36% of the time, Pallas kernels for 0%

commit v1 on v0

--- a/solution.py
+++ b/solution.py
@@ -98,7 +98,7 @@
             rows_all, heads_here, head_dim
         )
         local_fast = fast_init[layer]
-        full_fast = lax.all_gather(local_fast, "view", axis=3, tiled=True)
+        full_fast = jnp.concatenate(lax.all_gather(local_fast, "view"), axis=3)
 
         def accumulate(total, inputs):
             return (total + fast_gradient(inputs[0], inputs[1], inputs[2], full_fast), None)

time: 649 us -> 630 us (0.971); the launches traced: 637 us -> 625 us
  matrix products: 294 us -> 277 us
  waiting for transfers between devices: 130 us -> 139 us
    dot_general x8, matrix products: 24.3 us -> 11.8 us  [fast_gradient(): jnp.einsum('thd,thf->hdf', target, hidden, preferred_element_type=jnp.flo...]
    all_gather x4 -> x0, local copies, waits for them, and re-layouts: 12.4 us -> none  [shards(): full_fast = lax.all_gather(local_fast, 'view', axis=3, tiled=True)]
    psum x2, waiting for transfers between devices: 52.8 us -> 64.1 us  [shards(): lax.psum(gradients.astype(jnp.bfloat16), 'view').astype(jnp.float32)]
    reshape x0 -> x4, local copies, waits for them, and re-layouts: none -> 10.9 us  [shards(): full_fast = jnp.concatenate(lax.all_gather(local_fast, 'view'), axis=3)]
    dot_general x8, matrix products: 13.7 us -> 6.11 us  [fast_gradient(): jnp.einsum('thd,hdf->thf', target, weights[:, 2], preferred_element_type=...]
where the time goes in v1:
time: 630 us; the launch traced here: 625 us
  matrix products  277 us (44%)
  waiting for transfers between devices  139 us (22%)
  blocking collectives  80 us (13%)
  local copies, waits for them, and re-layouts  55.9 us (9%)
  other arithmetic  49.6 us (8%)
  between operations  14.4 us (2%)
  starting transfers between devices  7.59 us (1%)
    all_gather x2, blocking collectives, shards(): full_fast = jnp.concatenate(lax.all_gather(local_fast, 'view'), axis=3)  80 us
    psum x2, waiting for transfers between devices, shards(): lax.psum(gradients.astype(jnp.bfloat16), 'view').astype(jnp.float32)  64.1 us
    all_gather x2, waiting for transfers between devices, shards(): whole = lax.all_gather(normed, 'head', axis=0, tiled=True)  38.5 us
    dot_general x8, matrix products, fast_apply(): jnp.einsum('thf,hdf->thd', hidden, weights[:, 2], preferred_element_type=...  33 us
    dot_general x8, matrix products, attend_block(): jnp.einsum('vqhd,vkhd->vhqk', query_block, key_views, preferred_element_t...  32.3 us
    dot_general x8, matrix products, fast_apply(): jnp.einsum('thd,hdf->thf', queries, weights[:, 0], preferred_element_type...  30 us
    dot_general x8, matrix products, attend_block(): jnp.einsum('vhqk,vkhd->vqhd', probs, value_views, preferred_element_type=...  29.3 us
    all_to_all x2, waiting for transfers between devices, shards(): lax.all_to_all(mixed, 'head', split_axis=0, concat_axis=1, tiled=True)  28.7 us
  transfers between devices with their start and end apart: 10, of which 7 were waited for; matrix products, arithmetic and copies ran while one was open for 36% of the time, Pallas kernels for 0%

profile of v1, /device:TPU:0, one launch (start us, length us, event | category | flops | bytes accessed | tf_op | source)
XLA Modules:
  0.0 624.7 jit_solution(1465987934055149510)
XLA Ops:
  12.7 42.3 %all_gather.26 = bf16[8,4,3,64,64]{4,3,2,1,0:T(8,128)(2,1)S(1)} all-gather(bf16[1,4,3,64,64]{4,3,2,1,0:T(8,128)(2,1)S(1)} %get-tuple-element.358), channel_id=1, replica_groups=mesh['view'=8,'head'=4] {'view'}, dimensions={0}, use_global_device_ids=true | all-gather | bytes 884736 | tf_op jit(solution)/shard_map/all_gather | solution.py:101
  60.4 6.5 %all-gather.15.cloned.1.call-done = bf16[1,3,1024,256]{2,3,1,0:T(8,128)(2,1)} async-done(((bf16[1,3,128,256]{2,3,1,0:T(8,128)(2,1)}), bf16[1,3,1024,256]{2,3,1,0:T(8,128)(2,1)}) %all-gather.15.cloned.1.call-update) | async-done | bytes 1572880 | tf_op jit(solution)/shard_map/all_gather | solution.py:71
  66.9 35.3 %all-gather.11.cloned.1.call-done = bf16[2048,1024]{1,0:T(8,128)(2,1)} async-done(((bf16[512,1024]{1,0:T(8,128)(2,1)}), bf16[2048,1024]{1,0:T(8,128)(2,1)}) %all-gather.11.cloned.1.call-update) | async-done | bytes 4194320 | tf_op jit(solution)/shard_map/all_gather | solution.py:67
  102.2 6.1 fusion.188
  123.1 53.5 %while.66 = (s32[]{:T(128)}, f32[4,3,64,512]{3,2,0,1:T(8,128)S(1)}, bf16[4,512,4,64]{1,3,2,0:T(8,128)(2,1)}, s32[4,512]{1,0:T(4,128)S(1)}, bf16[4,512,4,64]{1,3,...) while((s32[]{:T(128)}, f32[4,3,64,512]{3,2,0,1:T(8,128)S(1)}, ...), condition=%wide.region_7.8_spmd.clone, body=%wide.region_6.7_spmd.clone.sunk | while | flops 830996992 | bytes 54796444 | solution.py:108
  189.8 31.0 %while.62 = (s32[]{:T(128)}, f32[4,1,512,4,64]{2,4,3,1,0:T(8,128)S(1)}, bf16[4,1,512,4,64]{2,4,3,1,0:T(8,128)(2,1)}, bf16[1,2048,4,64]{1,3,2,0:T(8,128)(2,1)S(1)}, bf16[1,2048,4,64]{1,3,2,0:T(8,128)(2,1)}, /*index=5*/s32[]{:T(128)}) while((s32[]{:T(128)}, f32[4,1,512,4,64]{2,4,3,1,0:T(8,128)S(1)}, bf16[4,1,512,4,64]{2,4,3,1,0:T(8,128)(2,1)}, ...), condition=%wide.region_5.6_spmd, body=%wide.region_3.5_spmd.sunk | while | flops 1094711296 | bytes 40648816 | solution.py:97
  189.8 4.0 fusion.368
  197.5 4.0 fusion.368
  205.3 4.0 fusion.368
  213.0 4.0 fusion.368
  220.8 32.2 %all-reduce.3.cloned.1.call-done = bf16[4,3,64,512]{3,2,1,0:T(8,128)(2,1)} async-done(((bf16[4,3,64,512]{3,2,1,0:T(8,128)(2,1)}), bf16[4,3,64,512]{3,2,1,0:T(8,128)(2,1)}) %all-reduce.3.cloned.1.call-update) | async-done | bytes 786448 | tf_op jit(solution)/shard_map/psum | solution.py:113
  277.4 35.6 %while.63 = (s32[]{:T(128)}, f32[4,512,4,64]{1,3,2,0:T(8,128)}, bf16[4,512,4,64]{1,3,2,0:T(8,128)(2,1)}, bf16[4,3,64,512]{3,2,0,1:T(8,128)(2,1)}, s32[]{:T(128)}) while((s32[]{:T(128)}, f32[4,512,4,64]{1,3,2,0:T(8,128)}, bf16[4,512,4,64]{1,3,2,0:T(8,128)(2,1)}, bf16[4,3,64,512]{3,2,0,1:T(8,128)(2,1)}, s32[]{:T(128)}) %tuple.131), condition=%wide.region_12.13_spmd, body=%wide.region_10.12_spmd.sunk | while | flops 409339904 | bytes 11305041 | solution.py:123
  281.2 4.2 multiply_reduce_fusion.8
  290.1 4.2 multiply_reduce_fusion.8
  299.0 4.2 multiply_reduce_fusion.8
  307.9 4.2 multiply_reduce_fusion.8
  319.6 14.3 %all-to-all-done = bf16[4,512,256]{1,2,0:T(8,128)(2,1)S(1)} async-done(((bf16[4,512,256]{1,2,0:T(8,128)(2,1)}), bf16[4,512,256]{1,2,0:T(8,128)(2,1)S(1)}, u32[]{:S(2)}, u32[]{:S(2)}) %all-to-all-start) | async-done | bytes 1048608 | tf_op jit(solution)/shard_map/all_to_all | solution.py:127
  339.3 37.7 %all_gather.30 = bf16[8,4,3,64,64]{4,3,2,1,0:T(8,128)(2,1)S(1)} all-gather(bf16[1,4,3,64,64]{4,3,2,1,0:T(8,128)(2,1)S(1)} %copy-done.23), channel_id=1, replica_groups=mesh['view'=8,'head'=4] {'view'}, dimensions={0}, use_global_device_ids=true | all-gather | bytes 884736 | tf_op jit(solution)/shard_map/all_gather | solution.py:101
  385.9 6.1 fusion.191
  406.6 56.0 %while.67 = (s32[]{:T(128)}, f32[4,3,64,512]{3,2,0,1:T(8,128)S(1)}, bf16[4,512,4,64]{1,3,2,0:T(8,128)(2,1)}, s32[4,512]{1,0:T(4,128)}, bf16[4,512,4,64]{1,3,2,0:...) while((s32[]{:T(128)}, f32[4,3,64,512]{3,2,0,1:T(8,128)S(1)}, ...), condition=%wide.region_20.21_spmd.clone, body=%wide.region_19.20_spmd.clone.sunk | while | flops 830996992 | bytes 54796444 | solution.py:108
  476.1 31.0 %while.64 = (s32[]{:T(128)}, f32[4,1,512,4,64]{2,4,3,1,0:T(8,128)S(1)}, bf16[4,1,512,4,64]{2,4,3,1,0:T(8,128)(2,1)}, bf16[1,2048,4,64]{1,3,2,0:T(8,128)(2,1)S(1)}, bf16[1,2048,4,64]{1,3,2,0:T(8,128)(2,1)}, /*index=5*/s32[]{:T(128)}) while((s32[]{:T(128)}, f32[4,1,512,4,64]{2,4,3,1,0:T(8,128)S(1)}, bf16[4,1,512,4,64]{2,4,3,1,0:T(8,128)(2,1)}, ...), condition=%wide.region_18.19_spmd, body=%wide.region_16.18_spmd.sunk | while | flops 1094711296 | bytes 40648816 | solution.py:97
  476.1 4.0 fusion.376
  483.9 4.0 fusion.376
  491.7 4.0 fusion.376
  499.4 4.0 fusion.376
  507.2 31.9 %all-reduce.5.cloned.1.call-done = bf16[4,3,64,512]{3,2,1,0:T(8,128)(2,1)} async-done(((bf16[4,3,64,512]{3,2,1,0:T(8,128)(2,1)}), bf16[4,3,64,512]{3,2,1,0:T(8,128)(2,1)}) %all-reduce.5.cloned.1.call-update) | async-done | bytes 786448 | tf_op jit(solution)/shard_map/psum | solution.py:113
  561.2 31.5 %while.65 = (s32[]{:T(128)}, f32[4,512,4,64]{1,3,2,0:T(8,128)S(1)}, bf16[4,512,4,64]{1,3,2,0:T(8,128)(2,1)}, bf16[4,3,64,512]{3,2,0,1:T(8,128)(2,1)S(1)}, s32[]{:T(128)}) while((s32[]{:T(128)}, f32[4,512,4,64]{1,3,2,0:T(8,128)S(1)}, bf16[4,512,4,64]{1,3,2,0:T(8,128)(2,1)}, bf16[4,3,64,512]{3,2,0,1:T(8,128)(2,1)S(1)}, s32[]{:T(128)}) %tuple.140), condition=%wide.region_25.26_spmd, body=%wide.region_23.25_spmd.sunk | while | flops 409339904 | bytes 11305041 | solution.py:123
  564.9 4.1 multiply_reduce_fusion.9
  572.8 4.1 multiply_reduce_fusion.9
  580.6 4.1 multiply_reduce_fusion.9
  588.6 4.1 multiply_reduce_fusion.9
  599.5 14.4 %all-to-all-done.1 = bf16[4,512,256]{1,2,0:T(8,128)(2,1)S(1)} async-done(((bf16[4,512,256]{1,2,0:T(8,128)(2,1)}), bf16[4,512,256]{1,2,0:T(8,128)(2,1)S(1)}, u32[]{:S(2)}, u32[]{:S(2)}) %all-to-all-start.1) | async-done | bytes 1048608 | tf_op jit(solution)/shard_map/all_to_all | solution.py:127
  (300 shorter events, 316.6 us)
Async XLA Ops:
  6.5 2.7 copy-start.15
  6.5 60.4 %all-gather.15.cloned.1.call-start = ((), (), s32[]{:S(2)}) async-start(), calls=%async_computation.6 | async-start | bytes 1769472 | tf_op jit(solution)/shard_map/all_gather | solution.py:71
  9.2 2.8 copy-start.26
  9.2 93.0 %all-gather.11.cloned.1.call-start = ((), (), s32[]{:S(2)}) async-start(), calls=%async_computation.2 | async-start | bytes 5242880 | tf_op jit(solution)/shard_map/all_gather | solution.py:67
  10.8 242.2 %all-reduce.3.cloned.1.call-start = ((), (), s32[]{:S(2)}) async-start(), calls=%async_computation.3 | async-start | bytes 1572864 | tf_op jit(solution)/shard_map/psum | solution.py:113
  60.3 48.0 %copy-start.9 = (bf16[4,3,64,512]{3,2,1,0:T(8,128)(2,1)}, bf16[4,3,64,512]{3,2,1,0:T(8,128)(2,1)S(1)}, u32[]{:S(2)}) copy-start(bf16[4,3,64,512]{3,2,1,0:T(8,128)(2,1)S(1)} %reshape.327) | copy-start | bytes 2359300
  108.4 3.3 copy-start.2
  177.7 141.9 %all-gather.17.cloned.1.call-start = ((), (), s32[]{:S(2)}) async-start(), calls=%async_computation.7 | async-start | bytes 2359296 | tf_op jit(solution)/shard_map/all_gather | solution.py:130
  178.6 204.1 %all-gather.19.cloned.1.call-start = ((), (), s32[]{:S(2)}) async-start(), calls=%async_computation.8 | async-start | bytes 1769472 | tf_op jit(solution)/shard_map/all_gather | solution.py:71
  189.8 4.1 copy-start.19
  197.5 4.1 copy-start.19
  205.3 4.1 copy-start.19
  213.0 4.1 copy-start.19
  253.0 5.2 copy-start.17
  315.9 18.1 %copy-start.16 = (bf16[512,1024]{1,0:T(8,128)(2,1)S(1)}, bf16[512,1024]{1,0:T(8,128)(2,1)}, u32[]{:S(2)}) copy-start(bf16[512,1024]{1,0:T(8,128)(2,1)} %param.17) | copy-start | bytes 3145732
  315.9 18.1 %all-to-all-start = ((bf16[4,512,256]{1,2,0:T(8,128)(2,1)}), bf16[4,512,256]{1,2,0:T(8,128)(2,1)S(1)}, u32[]{:S(2)}, u32[]{:S(2)}) async-start(bf16[4,512,256]{1,2,0:T(8,128)(2,1)} %fusion.206), calls=%async_computation | async-start | bytes 2097152 | tf_op jit(solution)/shard_map/all_to_all | solution.py:127
  319.5 66.3 %all-gather.13.cloned.1.call-start = ((), (), s32[]{:S(2)}) async-start(), calls=%async_computation.4 | async-start | bytes 5242880 | tf_op jit(solution)/shard_map/all_gather | solution.py:67
  339.2 199.8 %all-reduce.5.cloned.1.call-start = ((), (), s32[]{:S(2)}) async-start(), calls=%async_computation.5 | async-start | bytes 1572864 | tf_op jit(solution)/shard_map/psum | solution.py:113
  382.6 9.4 %copy-start.11 = (bf16[4,3,64,512]{3,2,1,0:T(8,128)(2,1)}, bf16[4,3,64,512]{3,2,1,0:T(8,128)(2,1)S(1)}, u32[]{:S(2)}) copy-start(bf16[4,3,64,512]{3,2,1,0:T(8,128)(2,1)S(1)} %reshape.332) | copy-start | bytes 2359300
  392.0 3.2 copy-start.3
  422.3 2.5 copy-start.13
  450.2 2.5 copy-start.13
  463.7 135.8 %all-gather.21.cloned.1.call-start = ((), (), s32[]{:S(2)}) async-start(), calls=%async_computation.9 | async-start | bytes 2359296 | tf_op jit(solution)/shard_map/all_gather | solution.py:130
  464.4 3.9 copy-start.1
  476.1 4.1 copy-start.20
  483.9 4.1 copy-start.20
  491.6 4.1 copy-start.20
  499.4 4.1 copy-start.20
  507.1 38.8 %copy-start.8 = (f32[4,1,512,4,64]{2,4,3,1,0:T(8,128)}, f32[4,1,512,4,64]{2,4,3,1,0:T(8,128)S(1)}, u32[]{:S(2)}) copy-start(f32[4,1,512,4,64]{2,4,3,1,0:T(8,128)S(1)} %get-tuple-element.170) | copy-start | bytes 6291460
  539.0 5.2 copy-start.18
  595.8 18.1 %copy-start.22 = (bf16[512,1024]{1,0:T(8,128)(2,1)S(1)}, bf16[512,1024]{1,0:T(8,128)(2,1)}, u32[]{:S(2)}) copy-start(bf16[512,1024]{1,0:T(8,128)(2,1)} %copy-done.21) | copy-start | bytes 3145732
  595.8 18.1 %all-to-all-start.1 = ((bf16[4,512,256]{1,2,0:T(8,128)(2,1)}), bf16[4,512,256]{1,2,0:T(8,128)(2,1)S(1)}, u32[]{:S(2)}, u32[]{:S(2)}) async-start(bf16[4,512,256]{1,2,0:T(8,128)(2,1)} %fusion.202), calls=%async_computation.1 | async-start | bytes 2097152 | tf_op jit(solution)/shard_map/all_to_all | solution.py:127
  (19 other events, 36.2 us)
Sparse Core Ops, SparseCore 0:
  9.4 57.5 all-gather.14
  68.5 33.6 all-gather.10
  177.8 75.1 all-reduce.2
  255.0 48.2 all-gather.16
  305.1 45.6 all-gather.18
  352.2 33.5 all-gather.12
  463.8 75.2 all-reduce.4
  541.2 48.2 all-gather.20
